TPU v7x, 32 devices: a whole 2x2x4 slice. The times are simulated.
32 devices in a mesh: blk: 8 (over z, x), rep: 4 (over y, core).
Axes of the slice: x: 2, y: 2, z: 4, core: 2. Of those that a mesh axis runs over, the one named last changes fastest.
Arguments:
- features: bfloat16 [32768, 128], P('blk'), may hold values from -6 to 6
- weight: bfloat16 [128, 256], replicated, may hold values from -0.5 to 0.5
- bias: float32 [256], replicated, may hold values from -3 to 3
- tile_values: bfloat16 [8, 8, 160, 128, 128], P('blk', 'rep'), may hold values from 0 to 0.041748047
- tile_place: int32 [8, 8, 160], P('blk', 'rep'), may hold values from 0 to 1023, as said below
- tile_count: int32 [8, 8], P('blk', 'rep'), may hold values from 1 to 160, as said below
Outputs:
- activations: bfloat16 [32768, 256], P('blk')
Inputs may be any that keep to these rules, and one draw needn't show every extreme that they name: `tile_place`: within one pair of destination block and section the 160 positions are distinct. `tile_count`: some pair of destination block and section has all 160 slots occupied.
All inputs are finite; a program needn't handle non-finite values.
Results may differ from a plain program's by a relative error of at most 0.0046.
Values may be sent and summed in bfloat16 or wider, within the bound.
A program may use at most 128 MiB of HBM per device.

v0:
```python
import jax
import jax.numpy as jnp
from jax import lax
from jax.sharding import PartitionSpec as P

TILE = 128


def section_terms(source, tiles, place, count):
    row_count = source.shape[0]
    row_tiles = row_count // TILE
    column = place % row_tiles
    target = place // row_tiles
    blocked = source.reshape(row_tiles, TILE, source.shape[1])
    pieces = jnp.take(blocked, column, axis=0)
    products = jnp.einsum("kij,kjf->kif", tiles, pieces, preferred_element_type=jnp.float32)
    slot_ids = jnp.arange(place.shape[0], dtype=jnp.int32)
    live = (slot_ids < count).astype(jnp.float32)
    products = products * live[:, None, None]
    summed = jax.ops.segment_sum(products, target, num_segments=row_tiles)
    return summed.reshape(row_count, source.shape[1])


def shards(features, weight, bias, tile_values, tile_place, tile_count):
    row_count = features.shape[0]
    sections = tile_values.shape[1]
    cycle_size = lax.axis_size("blk")
    my_replica = lax.axis_index("rep")
    partial_value = jnp.zeros((row_count, features.shape[1]), jnp.float32)
    piece_rows = row_count // cycle_size
    pieces = features.reshape(cycle_size, piece_rows, features.shape[1])
    holding = lax.all_to_all(pieces, "blk", split_axis=0, concat_axis=0, tiled=True)
    for section_index in range(sections):
        offset = my_replica * sections + section_index
        rolled = jnp.roll(holding, offset, axis=0)
        arrived = lax.all_to_all(rolled, "blk", split_axis=0, concat_axis=0, tiled=True)
        source = arrived.reshape(row_count, features.shape[1])
        partial_value = partial_value + section_terms(
            source,
            tile_values[0, section_index],
            tile_place[0, section_index],
            tile_count[0, section_index],
        )
    summed = lax.psum(partial_value, "rep")
    aggregated = summed.astype(jnp.bfloat16)
    output = jnp.dot(aggregated, weight, preferred_element_type=jnp.float32) + bias
    return jnp.maximum(output, 0.0).astype(jnp.bfloat16)


def solution(mesh):
    in_specs = (
        P("blk", None),
        P(),
        P(),
        P("blk", "rep", None, None, None),
        P("blk", "rep", None),
        P("blk", "rep"),
    )
    out_specs = P("blk", None)
    return jax.shard_map(shards, mesh=mesh, in_specs=in_specs, out_specs=out_specs, check_vma=False)
```

profile of v0, /device:TPU:1, one launch (start us, length us, event | category | flops | bytes accessed | tf_op | source)
XLA Modules:
  0.0 222.3 jit_solution(2415213686946378558)
XLA Ops:
  0.0 0.0 copy-start
  0.0 6.5 %all-to-all-start = ((bf16[8,512,128]{2,1,0:T(8,128)(2,1)}), bf16[8,512,128]{2,1,0:T(8,128)(2,1)S(1)}, u32[]{:S(2)}, u32[]{:S(2)}) async-start(bf16[8,512,128]{2,1,0:T(8,128)(2,1)} %bitcast.45), calls=%async_computation | async-start | bytes 2097152 | tf_op jit(solution)/shard_map/all_to_all | solution.py:32
  6.5 25.0 %all-to-all-done = bf16[8,512,128]{2,1,0:T(8,128)(2,1)S(1)} async-done(((bf16[8,512,128]{2,1,0:T(8,128)(2,1)}), bf16[8,512,128]{2,1,0:T(8,128)(2,1)S(1)}, u32[]{:S(2)}, u32[]{:S(2)}) %all-to-all-start) | async-done | bytes 1048608 | tf_op jit(solution)/shard_map/all_to_all | solution.py:32
  31.4 0.1 constant_dynamic-update-slice_fusion.1
  31.5 0.0 copy-start.2
  31.5 0.0 copy-start.3
  31.5 0.1 constant_dynamic-update-slice_fusion
  31.7 1.1 constant_dynamic-slice_fusion
  32.8 29.1 %all_to_all.15 = bf16[8,512,128]{2,1,0:T(8,128)(2,1)S(1)} all-to-all(bf16[8,512,128]{2,1,0:T(8,128)(2,1)S(1)} %get-tuple-element.11), channel_id=1, replica_groups=mesh['blk'=8,'rep'=4] {'blk'}, dimensions={0} | all-to-all | bytes 2097152 | tf_op jit(solution)/shard_map/all_to_all | solution.py:36
  61.9 4.3 %all-to-all-start.1 = ((bf16[8,512,128]{2,1,0:T(8,128)(2,1)}), bf16[8,512,128]{2,1,0:T(8,128)(2,1)S(1)}, u32[]{:S(2)}, u32[]{:S(2)}) async-start(bf16[8,512,128]{2,1,0:T(8,128)(2,1)} %get-tuple-element.12), calls=%async_computation.1 | async-start | bytes 2097152 | tf_op jit(solution)/shard_map/all_to_all | solution.py:36
  66.2 0.0 copy-done.2
  66.2 0.0 copy-done.3
  66.2 0.7 fusion.28
  66.9 0.7 compare_and_fusion
  67.6 0.6 compare_and_fusion.1
  68.2 7.7 %gather_fusion.1 = bf16[160,128,128]{2,1,0:T(8,128)(2,1)} fusion(bf16[32,128,128]{2,1,0:T(8,128)(2,1)S(1)} %bitcast.43, s32[1024]{0:T(1024)S(1)} %pad_clamp_fusion), kind=kCustom, calls=%fused_computation.1.clone | custom fusion | bytes 10486400 | tf_op jit(solution)/shard_map/jit(_take)/gather | solution.py:15
  75.9 11.8 %multiply_bitcast_fusion = f32[160,128,128]{1,2,0:T(8,128)} fusion(f32[160]{0:T(256)S(1)} %get-tuple-element.20, bf16[1,2,160,128,128]{4,3,2,1,0:T(8,128)(2,1)} %param.13, bf16[160,128,128]{2,1,0:T(8,128)(2,1)} %gather_fusion.1, pred[160]{0:T(512)(128)(4,1)S(1)} %get-tuple-element.6), kind=kOutput, calls=%fused_computation.4 | convolution fusion | flops 676331520 | bytes 20972320 | tf_op jit(solution)/shard_map/kij,kjf->kif/dot_general | solution.py:16
  87.7 11.7 %copy.12 = f32[160,128,128]{2,1,0:T(8,128)} copy(f32[160,128,128]{1,2,0:T(8,128)} %multiply_bitcast_fusion) | data formatting | bytes 20971520 | tf_op jit(solution)/shard_map/mul | solution.py:19
  99.5 0.0 all-to-all-done.1
  99.5 7.7 %gather_fusion = bf16[160,128,128]{2,1,0:T(8,128)(2,1)} fusion(bf16[32,128,128]{2,1,0:T(8,128)(2,1)S(1)} %bitcast.42, s32[1024]{0:T(1024)S(1)} %pad_clamp_fusion.1), kind=kCustom, calls=%fused_computation.clone | custom fusion | bytes 10486400 | tf_op jit(solution)/shard_map/jit(_take)/gather | solution.py:15
  107.2 11.8 %multiply_bitcast_fusion.1 = f32[160,128,128]{1,2,0:T(8,128)} fusion(f32[160]{0:T(256)S(1)} %get-tuple-element.19, bf16[1,2,160,128,128]{4,3,2,1,0:T(8,128)(2,1)} %param.13, bf16[160,128,128]{2,1,0:T(8,128)(2,1)} %gather_fusion, pred[160]{0:T(512)(128)(4,1)S(1)} %get-tuple-element.9), kind=kOutput, calls=%fused_computation.5 | convolution fusion | flops 676331520 | bytes 20972320 | tf_op jit(solution)/shard_map/kij,kjf->kif/dot_general | solution.py:16
  119.0 11.7 %copy.10 = f32[160,128,128]{2,1,0:T(8,128)} copy(f32[160,128,128]{1,2,0:T(8,128)} %multiply_bitcast_fusion.1) | data formatting | bytes 20971520 | tf_op jit(solution)/shard_map/mul | solution.py:19
  130.7 0.2 broadcast.127.clone.1
  131.0 21.2 %scatter_fusion.1 = f32[32,128,128]{2,1,0:T(8,128)S(1)} fusion(f32[32,128,128]{2,1,0:T(8,128)S(1)} %broadcast.127.clone.1, s32[160]{0:T(256)S(1)} %bitcast.47, f32[160,128,128]{2,1,0:T(8,128)} %copy.12), kind=kCustom, calls=%fused_computation.3 | custom fusion | flops 2621440 | bytes 31457920 | tf_op jit(solution)/shard_map/scatter-add | solution.py:20
  152.2 0.0 copy-start.1
  152.2 1.3 copy-done.1
  153.5 0.2 broadcast.127.clone
  153.7 21.2 %scatter_fusion = f32[32,128,128]{2,1,0:T(8,128)S(1)} fusion(f32[32,128,128]{2,1,0:T(8,128)S(1)} %broadcast.127.clone, s32[160]{0:T(256)S(1)} %bitcast.46, f32[160,128,128]{2,1,0:T(8,128)} %copy.10), kind=kCustom, calls=%fused_computation.2 | custom fusion | flops 2621440 | bytes 31457920 | tf_op jit(solution)/shard_map/scatter-add | solution.py:20
  174.9 0.0 copy-start.4
  174.9 3.2 %add.66 = f32[32,128,128]{2,1,0:T(8,128)} add(f32[32,128,128]{2,1,0:T(8,128)S(1)} %scatter_fusion, f32[32,128,128]{2,1,0:T(8,128)} %copy-done.1) | non-fusion elementwise | flops 524288 | bytes 6291456 | tf_op jit(solution)/shard_map/add | solution.py:38
  178.1 42.2 %all-reduce.1 = bf16[4096,128]{1,0:T(8,128)(2,1)S(1)} all-reduce(f32[4096,128]{1,0:T(8,128)} %bitcast.44), channel_id=1, replica_groups=mesh['blk'=8,'rep'=4] {'rep'}, use_global_device_ids=true, to_apply=%region_2.5 | all-reduce | flops 524288 | bytes 3145728 | tf_op jit(solution)/shard_map/psum | solution.py:44
  220.3 0.0 copy-done
  220.3 0.0 copy-done.4
  220.3 2.0 fusion.11
  (4 shorter events, 0.0 us)
Async XLA Ops:
  0.0 220.3 %copy-start = (bf16[128,256]{1,0:T(8,128)(2,1)S(1)}, bf16[128,256]{1,0:T(8,128)(2,1)}, u32[]{:S(2)}) copy-start(bf16[128,256]{1,0:T(8,128)(2,1)} %param.11) | copy-start | bytes 196612
  0.0 31.4 %all-to-all-start = ((bf16[8,512,128]{2,1,0:T(8,128)(2,1)}), bf16[8,512,128]{2,1,0:T(8,128)(2,1)S(1)}, u32[]{:S(2)}, u32[]{:S(2)}) async-start(bf16[8,512,128]{2,1,0:T(8,128)(2,1)} %bitcast.45), calls=%async_computation | async-start | bytes 2097152 | tf_op jit(solution)/shard_map/all_to_all | solution.py:32
  31.5 34.7 %copy-start.2 = (s32[1,2,160]{2,1,0:T(2,128)S(1)}, s32[1,2,160]{2,1,0:T(2,128)}, u32[]{:S(2)}) copy-start(s32[1,2,160]{2,1,0:T(2,128)} %param.14) | copy-start | bytes 3844
  31.5 34.7 %copy-start.3 = (s32[1,2]{1,0:T(1,128)S(1)}, s32[1,2]{1,0:T(1,128)}, u32[]{:S(2)}) copy-start(s32[1,2]{1,0:T(1,128)} %param.15) | copy-start | bytes 28
  61.9 37.5 %all-to-all-start.1 = ((bf16[8,512,128]{2,1,0:T(8,128)(2,1)}), bf16[8,512,128]{2,1,0:T(8,128)(2,1)S(1)}, u32[]{:S(2)}, u32[]{:S(2)}) async-start(bf16[8,512,128]{2,1,0:T(8,128)(2,1)} %get-tuple-element.12), calls=%async_computation.1 | async-start | bytes 2097152 | tf_op jit(solution)/shard_map/all_to_all | solution.py:36
  152.2 1.3 copy-start.1
  174.9 45.4 %copy-start.4 = (f32[256]{0:T(256)S(1)}, f32[256]{0:T(256)}, u32[]{:S(2)}) copy-start(f32[256]{0:T(256)} %param.12) | copy-start | bytes 3076
where the time goes:
time: 224 us; the launch traced here: 222 us
  blocking collectives  71.3 us (32%)
  other arithmetic  46.8 us (21%)
  local copies, waits for them, and re-layouts  42.7 us (19%)
  matrix products  25.7 us (11%)
  waiting for transfers between devices  25 us (11%)
  starting transfers between devices  10.7 us (5%)
    scatter-add x2, other arithmetic, section_terms(): summed = jax.ops.segment_sum(products, target, num_segments=row_tiles)  42.4 us
    psum x1, blocking collectives, shards(): summed = lax.psum(partial_value, 'rep')  42.2 us
    all_to_all x1, blocking collectives, shards(): lax.all_to_all(rolled, 'blk', split_axis=0, concat_axis=0, tiled=True)  29.1 us
    all_to_all x1, waiting for transfers between devices, shards(): lax.all_to_all(pieces, 'blk', split_axis=0, concat_axis=0, tiled=True)  25 us
    dot_general x2, matrix products, section_terms(): jnp.einsum('kij,kjf->kif', tiles, pieces, preferred_element_type=jnp.floa...  23.6 us
    mul x2, local copies, waits for them, and re-layouts, section_terms(): products = products * live[:, None, None]  23.5 us
    gather x2, local copies, waits for them, and re-layouts, section_terms(): pieces = jnp.take(blocked, column, axis=0)  15.4 us
    all_to_all x1, starting transfers between devices, shards(): lax.all_to_all(pieces, 'blk', split_axis=0, concat_axis=0, tiled=True)  6.47 us
  transfers between devices with their start and end apart: 2, of which 1 were waited for; matrix products, arithmetic and copies ran while one was open for 15% of the time, Pallas kernels for 0%

commit v1 on v0

--- a/solution.py
+++ b/solution.py
@@ -41,7 +41,7 @@
             tile_place[0, section_index],
             tile_count[0, section_index],
         )
-    summed = lax.psum(partial_value, "rep")
+    summed = jnp.sum(lax.all_gather(partial_value, "rep"), axis=0)
     aggregated = summed.astype(jnp.bfloat16)
     output = jnp.dot(aggregated, weight, preferred_element_type=jnp.float32) + bias
     return jnp.maximum(output, 0.0).astype(jnp.bfloat16)

time: 224 us -> 272 us (1.21)
  waiting for transfers between devices: 25 us -> 85.8 us
  blocking collectives: 71.3 us -> 29.1 us
  other arithmetic: 46.8 us -> 62.2 us
  between operations: 0.16 us -> 13.5 us
    all_gather x0 -> x1, waiting for transfers between devices: none -> 60.8 us  [shards(): summed = jnp.sum(lax.all_gather(partial_value, 'rep'), axis=0)]
    psum x1 -> x0, blocking collectives: 42.2 us -> none  [shards(): summed = lax.psum(partial_value, 'rep')]
    scatter-add x2, other arithmetic: 42.4 us -> 53.6 us  [section_terms(): summed = jax.ops.segment_sum(products, target, num_segments=row_tiles)]
    reduce_sum x0 -> x1, other arithmetic: none -> 4.13 us  [shards(): summed = jnp.sum(lax.all_gather(partial_value, 'rep'), axis=0)]
  transfers between devices with their start and end apart: 2 -> 3, of which waited for: 1 -> 2; matrix products, arithmetic and copies ran while one was open for 15% -> 12% of each run, Pallas kernels for 0% -> 0%
where the time goes in v1:
time: 272 us; the launch traced here: 270 us
  waiting for transfers between devices  85.8 us (32%)
  other arithmetic  62.2 us (23%)
  local copies, waits for them, and re-layouts  42.7 us (16%)
  blocking collectives  29.1 us (11%)
  matrix products  25.7 us (9%)
  between operations  13.5 us (5%)
  starting transfers between devices  10.8 us (4%)
    all_gather x1, waiting for transfers between devices, shards(): summed = jnp.sum(lax.all_gather(partial_value, 'rep'), axis=0)  60.8 us
    scatter-add x2, other arithmetic, section_terms(): summed = jax.ops.segment_sum(products, target, num_segments=row_tiles)  53.6 us
    all_to_all x1, blocking collectives, shards(): lax.all_to_all(rolled, 'blk', split_axis=0, concat_axis=0, tiled=True)  29.1 us
    all_to_all x1, waiting for transfers between devices, shards(): lax.all_to_all(pieces, 'blk', split_axis=0, concat_axis=0, tiled=True)  25 us
    dot_general x2, matrix products, section_terms(): jnp.einsum('kij,kjf->kif', tiles, pieces, preferred_element_type=jnp.floa...  23.7 us
    mul x2, local copies, waits for them, and re-layouts, section_terms(): products = products * live[:, None, None]  23.5 us
    gather x2, local copies, waits for them, and re-layouts, section_terms(): pieces = jnp.take(blocked, column, axis=0)  15.4 us
    all_to_all x1, starting transfers between devices, shards(): lax.all_to_all(pieces, 'blk', split_axis=0, concat_axis=0, tiled=True)  6.47 us
  transfers between devices with their start and end apart: 3, of which 2 were waited for; matrix products, arithmetic and copies ran while one was open for 12% of the time, Pallas kernels for 0%

profile of v1, /device:TPU:1, one launch (start us, length us, event | category | flops | bytes accessed | tf_op | source)
XLA Modules:
  0.0 269.8 jit_solution(15064016022891501216)
XLA Ops:
  6.5 0.0 copy-start
  6.5 6.5 %all-to-all-start = ((bf16[8,512,128]{2,1,0:T(8,128)(2,1)}), bf16[8,512,128]{2,1,0:T(8,128)(2,1)S(1)}, u32[]{:S(2)}, u32[]{:S(2)}) async-start(bf16[8,512,128]{2,1,0:T(8,128)(2,1)} %bitcast.45), calls=%async_computation | async-start | bytes 2097152 | tf_op jit(solution)/shard_map/all_to_all | solution.py:32
  13.0 25.0 %all-to-all-done = bf16[8,512,128]{2,1,0:T(8,128)(2,1)S(1)} async-done(((bf16[8,512,128]{2,1,0:T(8,128)(2,1)}), bf16[8,512,128]{2,1,0:T(8,128)(2,1)S(1)}, u32[]{:S(2)}, u32[]{:S(2)}) %all-to-all-start) | async-done | bytes 1048608 | tf_op jit(solution)/shard_map/all_to_all | solution.py:32
  38.0 0.1 constant_dynamic-update-slice_fusion.1
  38.0 0.0 copy-start.1
  38.1 0.0 copy-start.2
  38.1 0.1 constant_dynamic-update-slice_fusion
  38.2 1.1 constant_dynamic-slice_fusion
  39.3 29.1 %all_to_all.15 = bf16[8,512,128]{2,1,0:T(8,128)(2,1)S(1)} all-to-all(bf16[8,512,128]{2,1,0:T(8,128)(2,1)S(1)} %get-tuple-element.11), channel_id=1, replica_groups=mesh['blk'=8,'rep'=4] {'blk'}, dimensions={0} | all-to-all | bytes 2097152 | tf_op jit(solution)/shard_map/all_to_all | solution.py:36
  68.5 4.3 %all-to-all-start.1 = ((bf16[8,512,128]{2,1,0:T(8,128)(2,1)}), bf16[8,512,128]{2,1,0:T(8,128)(2,1)S(1)}, u32[]{:S(2)}, u32[]{:S(2)}) async-start(bf16[8,512,128]{2,1,0:T(8,128)(2,1)} %get-tuple-element.12), calls=%async_computation.1 | async-start | bytes 2097152 | tf_op jit(solution)/shard_map/all_to_all | solution.py:36
  72.7 0.0 all-gather.2.cloned.1.call-start
  72.8 0.0 copy-done.1
  72.8 0.0 copy-done.2
  72.8 0.7 fusion.28
  73.5 0.7 compare_and_fusion
  74.2 0.6 compare_and_fusion.1
  74.8 7.7 %gather_fusion.1 = bf16[160,128,128]{2,1,0:T(8,128)(2,1)} fusion(bf16[32,128,128]{2,1,0:T(8,128)(2,1)S(1)} %bitcast.43, s32[1024]{0:T(1024)S(1)} %pad_clamp_fusion), kind=kCustom, calls=%fused_computation.1.clone | custom fusion | bytes 10486400 | tf_op jit(solution)/shard_map/jit(_take)/gather | solution.py:15
  82.5 11.8 %multiply_bitcast_fusion = f32[160,128,128]{1,2,0:T(8,128)} fusion(f32[160]{0:T(256)S(1)} %get-tuple-element.20, bf16[1,2,160,128,128]{4,3,2,1,0:T(8,128)(2,1)} %param.13, bf16[160,128,128]{2,1,0:T(8,128)(2,1)} %gather_fusion.1, pred[160]{0:T(512)(128)(4,1)S(1)} %get-tuple-element.6), kind=kOutput, calls=%fused_computation.4 | convolution fusion | flops 676331520 | bytes 20972320 | tf_op jit(solution)/shard_map/kij,kjf->kif/dot_general | solution.py:16
  94.4 11.7 %copy.16 = f32[160,128,128]{2,1,0:T(8,128)} copy(f32[160,128,128]{1,2,0:T(8,128)} %multiply_bitcast_fusion) | data formatting | bytes 20971520 | tf_op jit(solution)/shard_map/mul | solution.py:19
  106.1 0.0 all-to-all-done.1
  106.1 7.7 %gather_fusion = bf16[160,128,128]{2,1,0:T(8,128)(2,1)} fusion(bf16[32,128,128]{2,1,0:T(8,128)(2,1)S(1)} %bitcast.42, s32[1024]{0:T(1024)S(1)} %pad_clamp_fusion.1), kind=kCustom, calls=%fused_computation.clone | custom fusion | bytes 10486400 | tf_op jit(solution)/shard_map/jit(_take)/gather | solution.py:15
  113.8 11.8 %multiply_bitcast_fusion.1 = f32[160,128,128]{1,2,0:T(8,128)} fusion(f32[160]{0:T(256)S(1)} %get-tuple-element.19, bf16[1,2,160,128,128]{4,3,2,1,0:T(8,128)(2,1)} %param.13, bf16[160,128,128]{2,1,0:T(8,128)(2,1)} %gather_fusion, pred[160]{0:T(512)(128)(4,1)S(1)} %get-tuple-element.9), kind=kOutput, calls=%fused_computation.5 | convolution fusion | flops 676331520 | bytes 20972320 | tf_op jit(solution)/shard_map/kij,kjf->kif/dot_general | solution.py:16
  125.6 11.7 %copy.14 = f32[160,128,128]{2,1,0:T(8,128)} copy(f32[160,128,128]{1,2,0:T(8,128)} %multiply_bitcast_fusion.1) | data formatting | bytes 20971520 | tf_op jit(solution)/shard_map/mul | solution.py:19
  137.4 0.2 broadcast.127.clone.1
  137.6 21.2 %scatter_fusion.1 = f32[32,128,128]{2,1,0:T(8,128)S(1)} fusion(f32[32,128,128]{2,1,0:T(8,128)S(1)} %broadcast.127.clone.1, s32[160]{0:T(256)S(1)} %bitcast.47, f32[160,128,128]{2,1,0:T(8,128)} %copy.16), kind=kCustom, calls=%fused_computation.3 | custom fusion | flops 2621440 | bytes 31457920 | tf_op jit(solution)/shard_map/scatter-add | solution.py:20
  158.8 1.6 broadcast.127.clone
  160.4 32.4 %scatter_fusion = f32[32,128,128]{2,1,0:T(8,128)} fusion(f32[32,128,128]{2,1,0:T(8,128)} %broadcast.127.clone, s32[160]{0:T(256)S(1)} %bitcast.46, f32[160,128,128]{2,1,0:T(8,128)} %copy.14), kind=kCustom, calls=%fused_computation.2 | custom fusion | flops 2621440 | bytes 31457920 | tf_op jit(solution)/shard_map/scatter-add | solution.py:20
  192.8 3.2 %add.71 = f32[32,128,128]{2,1,0:T(8,128)} add(f32[32,128,128]{2,1,0:T(8,128)} %scatter_fusion, f32[32,128,128]{2,1,0:T(8,128)S(1)} %scatter_fusion.1) | non-fusion elementwise | flops 524288 | bytes 6291456 | tf_op jit(solution)/shard_map/add | solution.py:38
  195.9 0.0 all-gather.2.cloned.1.call-update
  195.9 0.0 copy-start.3
  195.9 60.8 %all-gather.2.cloned.1.call-done = f32[4,4096,128]{2,1,0:T(8,128)} async-done(((f32[1,4096,128]{2,1,0:T(8,128)}), f32[4,4096,128]{2,1,0:T(8,128)}) %all-gather.2.cloned.1.call-update) | async-done | bytes 8388624 | tf_op jit(solution)/shard_map/all_gather | solution.py:44
  256.8 4.1 %reduce_sum.9 = bf16[4096,128]{1,0:T(8,128)(2,1)S(1)} reduce(f32[4,4096,128]{2,1,0:T(8,128)} %all-gather.2.cloned.1.call-done, f32[]{:T(128)} %constant.69.clone.1), dimensions={0}, to_apply=%region_2.5 | reduce | flops 1572864 | bytes 9437188 | tf_op jit(solution)/shard_map/reduce_sum | solution.py:44
  260.9 0.0 copy-done
  260.9 0.0 copy-done.3
  260.9 2.0 fusion.11
  (4 shorter events, 0.0 us)
Async XLA Ops:
  6.5 254.4 %copy-start = (bf16[128,256]{1,0:T(8,128)(2,1)S(1)}, bf16[128,256]{1,0:T(8,128)(2,1)}, u32[]{:S(2)}) copy-start(bf16[128,256]{1,0:T(8,128)(2,1)} %param.11) | copy-start | bytes 196612
  6.5 31.4 %all-to-all-start = ((bf16[8,512,128]{2,1,0:T(8,128)(2,1)}), bf16[8,512,128]{2,1,0:T(8,128)(2,1)S(1)}, u32[]{:S(2)}, u32[]{:S(2)}) async-start(bf16[8,512,128]{2,1,0:T(8,128)(2,1)} %bitcast.45), calls=%async_computation | async-start | bytes 2097152 | tf_op jit(solution)/shard_map/all_to_all | solution.py:32
  38.0 34.7 %copy-start.1 = (s32[1,2,160]{2,1,0:T(2,128)S(1)}, s32[1,2,160]{2,1,0:T(2,128)}, u32[]{:S(2)}) copy-start(s32[1,2,160]{2,1,0:T(2,128)} %param.14) | copy-start | bytes 3844
  38.1 34.7 %copy-start.2 = (s32[1,2]{1,0:T(1,128)S(1)}, s32[1,2]{1,0:T(1,128)}, u32[]{:S(2)}) copy-start(s32[1,2]{1,0:T(1,128)} %param.15) | copy-start | bytes 28
  68.5 37.6 %all-to-all-start.1 = ((bf16[8,512,128]{2,1,0:T(8,128)(2,1)}), bf16[8,512,128]{2,1,0:T(8,128)(2,1)S(1)}, u32[]{:S(2)}, u32[]{:S(2)}) async-start(bf16[8,512,128]{2,1,0:T(8,128)(2,1)} %get-tuple-element.12), calls=%async_computation.1 | async-start | bytes 2097152 | tf_op jit(solution)/shard_map/all_to_all | solution.py:36
  72.7 184.0 %all-gather.2.cloned.1.call-start = ((), (), s32[]{:S(2)}) async-start(), calls=%async_computation.3 | async-start | bytes 10485760 | tf_op jit(solution)/shard_map/all_gather | solution.py:44
  195.9 65.0 %copy-start.3 = (f32[256]{0:T(256)S(1)}, f32[256]{0:T(256)}, u32[]{:S(2)}) copy-start(f32[256]{0:T(256)} %param.12) | copy-start | bytes 3076
Sparse Core Ops, SparseCore 0:
  196.1 60.6 all-gather.1
